TPU v7x, 128 devices: a whole 4x4x4 slice. The times are simulated.
128 devices in a mesh: fibre: 32 (over y, z_lo, x), band: 4 (over z_hi, core).
Axes of the slice: x: 4, y: 4, z: 4 (z_hi: 2, z_lo: 2; z = z_hi * 2 + z_lo), core: 2. Of those that a mesh axis runs over, the one named last changes fastest.
Arguments:
- traces: bfloat16 [4096, 8192], P('fibre', 'band'), may hold values from -6 to 6
- alive: int32 [4096], P('fibre'), may hold values 0 or 1
- reach: int32 [4096], P('fibre'), may hold values from 1 to 128, as said below
Outputs:
- correlation: bfloat16 [128, 4096, 512], P(('fibre', 'band'))
Inputs may be any that keep to these rules, and one draw needn't show every extreme that they name: `reach`: each value is an offset limit of one channel; both 1 and 128 occur in every draw.
All inputs are finite; a program needn't handle non-finite values. No bound on the sum of `alive` on one device may be relied on, other than what follows from the above.
Results may differ from a plain program's by a relative error of at most 0.015.
Values may be sent and summed in bfloat16 or wider, within the bound.
No kernel may reach another device: no remote copies, remote signals or barrier semaphores. Data moves between devices by JAX's collectives and lax.ppermute only.
A program may use at most 192 MiB of HBM per device.

v0:
```python
import math

import jax
import jax.numpy as jnp
from jax import lax
from jax.sharding import PartitionSpec as P

NT = 8192
NF = 1024
HW = 32
OFFS = 128
LAGS = 512


epsilon = 1e-06


def with_halo(cells, sides, width):
    for axis, dim in sides:
        count = lax.axis_size(axis)
        ends = count - 1
        head = lax.slice_in_dim(cells, 0, width, axis=dim)
        tail = lax.slice_in_dim(cells, cells.shape[dim] - width, cells.shape[dim], axis=dim)
        cells = jnp.concatenate(
            [
                lax.ppermute(tail, axis, [(i, (i + 1) % count) for i in range(ends)]),
                cells,
                lax.ppermute(head, axis, [((i + 1) % count, i) for i in range(ends)]),
            ],
            axis=dim,
        )
    return cells


def passed_along(shard, axis, by):
    length = lax.axis_size(axis)
    pairs = [(i, i + by) for i in range(length) if 0 <= i + by < length]
    return lax.ppermute(shard, axis, pairs)


def trig_angles(freq_index, sample_index):
    phase = freq_index[:, None] * sample_index[None, :] % NT
    return phase.astype(jnp.float32) * (2.0 * math.pi / NT)


def lag_table():
    freq_index = jnp.arange(NF, dtype=jnp.int32)
    lag_index = (jnp.arange(LAGS, dtype=jnp.int32) - LAGS // 2) % NT
    angles = trig_angles(freq_index, lag_index)
    weights = jnp.where(freq_index == 0, 1.0, 2.0).astype(jnp.float32)[:, None]
    stacked = jnp.stack([weights * jnp.cos(angles), -weights * jnp.sin(angles)], axis=1)
    return stacked.reshape(2 * NF, LAGS).astype(jnp.bfloat16)


def window_matrix(row_total):
    row_index = jnp.arange(row_total, dtype=jnp.int32)[:, None]
    col_index = jnp.arange(row_total + 2 * HW, dtype=jnp.int32)[None, :]
    spread = col_index - row_index
    return ((spread >= 0) & (spread <= 2 * HW)).astype(jnp.float32)


def cross_pairs(whitened, neighbours, offsets, reach_values):
    width = whitened.shape[2]
    extended = jnp.concatenate([whitened, neighbours], axis=2)
    first = whitened.astype(jnp.float32)

    def one_offset(offset):
        partner = lax.dynamic_slice_in_dim(extended, offset + 1, width, 2).astype(jnp.float32)
        keep_mask = ((offset + 1).astype(jnp.float32) <= reach_values).astype(jnp.float32)
        real_part = (first[:, 0] * partner[:, 0] + first[:, 1] * partner[:, 1]) * keep_mask
        imag_part = (first[:, 1] * partner[:, 0] - first[:, 0] * partner[:, 1]) * keep_mask
        return jnp.stack([real_part, imag_part], axis=1).astype(jnp.bfloat16)

    return jax.vmap(one_offset)(offsets)


def to_lags(cross_spec):
    lag_basis = lag_table()
    flat = cross_spec.reshape(cross_spec.shape[0], 2 * NF, cross_spec.shape[3])
    lagged = jnp.einsum("ojc,jl->ocl", flat, lag_basis, preferred_element_type=jnp.float32)
    return (lagged * (1.0 / math.sqrt(NF))).astype(jnp.bfloat16)


def on_device(traces, alive, reach):
    channel_count = traces.shape[0]
    time_block = traces.shape[1]
    band_count = lax.axis_size("band")
    band_rank = lax.axis_index("band")
    local_nf = NF // band_count
    sample_index = band_rank * time_block + jnp.arange(time_block, dtype=jnp.int32)
    freq_index = jnp.arange(lax.axis_size("band") * local_nf, dtype=jnp.int32)
    angles = trig_angles(freq_index, sample_index)
    trig_table = jnp.stack([jnp.cos(angles), -jnp.sin(angles)], axis=1)
    trig_table = trig_table.reshape(2 * (lax.axis_size("band") * local_nf), time_block).astype(
        jnp.bfloat16
    )
    product = lax.dot_general(
        trig_table, traces, (((1,), (1,)), ((), ())), preferred_element_type=jnp.float32
    )
    spectrum = lax.psum_scatter(
        product.reshape(lax.axis_size("band") * local_nf, 2, channel_count),
        "band",
        scatter_dimension=0,
        tiled=True,
    )
    spec_power = spectrum[:, 0] * spectrum[:, 0] + spectrum[:, 1] * spectrum[:, 1]
    padded = with_halo(spec_power, (("band", 0),), HW)
    window_sum = jnp.dot(window_matrix(local_nf), padded, precision=lax.Precision.HIGHEST)
    centre = band_rank * local_nf + jnp.arange(local_nf, dtype=jnp.int32)
    counts = (jnp.minimum(centre + HW, NF - 1) - jnp.maximum(centre - HW, 0) + 1).astype(
        jnp.float32
    )
    scale = alive.astype(jnp.float32)[None, :] / jnp.sqrt(window_sum / counts[:, None] + epsilon)
    whitened = (spectrum * scale[:, None, :]).astype(jnp.bfloat16)
    neighbours = passed_along(whitened, "fibre", -1)
    cross_spec = cross_pairs(
        whitened, neighbours, jnp.arange(OFFS, dtype=jnp.int32), reach.astype(jnp.float32)
    )
    turned = lax.all_to_all(
        lax.all_to_all(cross_spec, "fibre", split_axis=0, concat_axis=3, tiled=True),
        "band",
        split_axis=0,
        concat_axis=1,
        tiled=True,
    )
    return to_lags(turned)


def solution(mesh):
    return jax.shard_map(
        on_device,
        mesh=mesh,
        in_specs=(P("fibre", "band"), P("fibre"), P("fibre")),
        out_specs=P(("fibre", "band"), None, None),
        check_vma=False,
    )
```

profile of v0, /device:TPU:10, one launch (start us, length us, event | category | flops | bytes accessed | tf_op | source)
XLA Modules:
  0.0 744.7 jit_solution(13869325913610723576)
XLA Ops:
  6.5 0.0 copy-start
  6.5 0.0 reduce-scatter.2.cloned.1.call-start
  6.5 34.0 %cosine_convert_fusion = (bf16[1024,1,2048]{2,0,1:T(8,128)(2,1)S(1)}, bf16[1024,1,2048]{2,0,1:T(8,128)(2,1)S(1)}) fusion(s32[2048]{0:T(1024)S(1)} %iota_add_fusion), kind=kLoop, calls=%fused_computation.16 | loop fusion | flops 35651584 | bytes 8396800 | tf_op jit(solution)/shard_map/convert.4
  40.6 0.0 copy-done
  40.6 0.0 copy-start.3
  40.6 0.0 copy-start.4
  40.6 3.3 fusion.3
  43.9 0.0 reduce-scatter.2.cloned.1.call-update
  43.9 0.0 copy-done.3
  44.0 0.0 copy-done.4
  44.0 0.1 compare_convert_fusion
  44.1 34.2 %reduce-scatter.2.cloned.1.call-done = f32[256,2,128]{2,0,1:T(8,128)} async-done(((f32[1024,2,128]{2,0,1:T(8,128)}), f32[256,2,128]{2,0,1:T(8,128)}) %reduce-scatter.2.cloned.1.call-update) | async-done | bytes 262160 | tf_op jit(solution)/shard_map/reduce_scatter | solution.py:100
  78.3 1.0 fusion.33
  79.3 1.7 collective-permute-start
  81.1 1.3 collective-permute-start.1
  82.4 1.0 fusion.47
  83.3 0.0 collective-permute-done
  83.4 0.9 collective-permute-done.1
  84.3 0.3 fusion.19
  84.6 1.0 fusion.44
  85.6 2.5 collective-permute-start.2
  88.1 0.1 copy.21
  88.2 0.1 copy.23
  88.3 4.1 collective-permute-done.2
  92.5 0.2 copy.22
  92.7 36.8 %gather_fusion = bf16[128,256,2,128]{1,2,3,0:T(2,128)(2,1)} fusion(bf16[256,2,256]{0,1,2:T(2,128)(2,1)S(1)} %copy.22, s32[128]{0:T(128)S(1)} %fusion.39), kind=kCustom, calls=%fused_computation | custom fusion | bytes 33555968 | tf_op jit(solution)/shard_map/vmap()/gather | solution.py:68
  129.5 17.5 %convert_element_type.91 = f32[128,256,2,128]{1,2,3,0:T(2,128)} convert(bf16[128,256,2,128]{1,2,3,0:T(2,128)(2,1)} %gather_fusion) | non-fusion elementwise | flops 8388608 | bytes 50331648 | tf_op jit(solution)/shard_map/vmap()/convert_element_type | solution.py:68
  147.0 58.4 %multiply_convert_fusion.1 = (bf16[128,256,1,128]{1,2,3,0:T(2,128)(2,1)S(1)}, bf16[128,256,1,128]{1,2,3,0:T(2,128)(2,1)}) fusion(f32[128,256,2,128]{1,2,3,0:T(2,128)} %convert_element_type.91, f32[128,128]{1,0:T(8,128)S(1)} %compare_convert_fusion, f32[256,128]{0,1:T(8,128)S(1)} %copy.23, f32[256,128]{0,1:T(8,128)S(1)} %copy.21), kind=kLoop, calls=%fused_computation.3 | loop fusion | flops 41943040 | bytes 50659328 | tf_op jit(solution)/shard_map/convert.2
  205.4 40.7 %pad_maximum_fusion = bf16[128,256,2,128]{1,2,3,0:T(2,128)(2,1)} fusion(bf16[128,256,1,128]{1,2,3,0:T(2,128)(2,1)} %get-tuple-element.8, bf16[128,256,1,128]{1,2,3,0:T(2,128)(2,1)S(1)} %get-tuple-element.7), kind=kLoop, calls=%fused_computation.1 | loop fusion | flops 33554432 | bytes 33554432 | tf_op jit(solution)/shard_map/vmap()/stack | solution.py:72
  246.1 194.6 %all_to_all.27 = bf16[128,256,2,128]{1,2,3,0:T(2,128)(2,1)S(1)} all-to-all(bf16[128,256,2,128]{1,2,3,0:T(2,128)(2,1)} %pad_maximum_fusion), channel_id=1, replica_groups=mesh['fibre'=32,'band'=4] {'fibre'}, dimensions={0} | all-to-all | bytes 33554432 | tf_op jit(solution)/shard_map/all_to_all | solution.py:120
  440.7 7.9 %copy.24 = bf16[32,4,256,2,128]{2,4,0,3,1:T(8,128)(2,1)} copy(bf16[32,4,256,2,128]{2,3,4,1,0:T(2,128)(2,1)S(1)} %bitcast.24) | data formatting | bytes 33554432 | tf_op jit(solution)/shard_map/all_to_all | solution.py:120
  448.6 23.8 %all-to-all-start.1 = ((bf16[4,256,2,4096]{1,3,2,0:T(8,128)(2,1)}), bf16[4,256,2,4096]{1,3,2,0:T(8,128)(2,1)}, u32[]{:S(2)}, u32[]{:S(2)}) async-start(bf16[4,256,2,4096]{1,3,2,0:T(8,128)(2,1)} %bitcast.23), calls=%async_computation.2 | async-start | bytes 33554432 | tf_op jit(solution)/shard_map/all_to_all | solution.py:119
  472.5 8.8 %multiply_convert_fusion.4 = (bf16[1024,1,512]{2,0,1:T(8,128)(2,1)S(1)}, bf16[1024,1,512]{2,0,1:T(8,128)(2,1)S(1)}) fusion(s32[512]{0:T(512)S(1)} %add_select_fusion.2, f32[1024]{0:T(1024)S(1)} %get-tuple-element.17, f32[1024]{0:T(1024)S(1)} %get-tuple-element.18), kind=kLoop, calls=%fused_computation.29 | loop fusion | flops 9437184 | bytes 2107392 | tf_op jit(solution)/shard_map/convert
  481.3 0.2 pad_maximum_fusion.1
  481.5 2.2 copy.26
  483.7 2.2 convert_element_type.96
  485.9 171.8 %all-to-all-done.1 = bf16[4,256,2,4096]{1,3,2,0:T(8,128)(2,1)} async-done(((bf16[4,256,2,4096]{1,3,2,0:T(8,128)(2,1)}), bf16[4,256,2,4096]{1,3,2,0:T(8,128)(2,1)}, u32[]{:S(2)}, u32[]{:S(2)}) %all-to-all-start.1) | async-done | bytes 16777248 | tf_op jit(solution)/shard_map/all_to_all | solution.py:119
  657.6 41.3 %copy.25 = bf16[4,256,2,4096]{3,2,1,0:T(2,128)(2,1)} copy(bf16[4,256,2,4096]{1,3,2,0:T(8,128)(2,1)} %all-to-all-done.1) | data formatting | bytes 33554432 | tf_op jit(solution)/shard_map/all_to_all | solution.py:119
  698.9 0.0 copy-start.2
  698.9 25.1 %reshape.348 = bf16[2048,4096]{1,0:T(8,128)(2,1)} reshape(bf16[4,256,2,4096]{3,2,1,0:T(2,128)(2,1)} %copy.25) | data formatting | bytes 33554432 | tf_op jit(solution)/shard_map/reshape.3
  724.0 0.0 copy-done.2
  724.0 0.0 copy-start.1
  724.0 13.9 %fusion.10 = bf16[1,4096,512]{2,1,0:T(8,128)(2,1)} fusion(bf16[2048,4096]{1,0:T(8,128)(2,1)} %reshape.348, bf16[2048,512]{1,0:T(8,128)(2,1)S(1)} %copy-done.2), kind=kOutput, calls=%fused_computation.20 | convolution fusion | flops 8594128896 | bytes 23068672 | tf_op jit(solution)/shard_map/ojc,jl->ocl/dot_general | solution.py:80
  737.9 0.0 copy-done.1
  (11 shorter events, 0.1 us)
Async XLA Ops:
  6.5 34.0 %copy-start = (bf16[128,2048]{1,0:T(8,128)(2,1)S(1)}, bf16[128,2048]{1,0:T(8,128)(2,1)}, u32[]{:S(2)}) copy-start(bf16[128,2048]{1,0:T(8,128)(2,1)} %param.3) | copy-start | bytes 1572868
  6.5 71.8 %reduce-scatter.2.cloned.1.call-start = ((), (), s32[]{:S(2)}) async-start(), calls=%async_computation.3 | async-start | bytes 1310720 | tf_op jit(solution)/shard_map/reduce_scatter | solution.py:100
  40.6 3.4 copy-start.3
  40.6 3.4 copy-start.4
  79.3 4.0 collective-permute-start
  81.1 3.2 collective-permute-start.1
  85.6 6.9 collective-permute-start.2
  448.6 209.0 %all-to-all-start.1 = ((bf16[4,256,2,4096]{1,3,2,0:T(8,128)(2,1)}), bf16[4,256,2,4096]{1,3,2,0:T(8,128)(2,1)}, u32[]{:S(2)}, u32[]{:S(2)}) async-start(bf16[4,256,2,4096]{1,3,2,0:T(8,128)(2,1)} %bitcast.23), calls=%async_computation.2 | async-start | bytes 33554432 | tf_op jit(solution)/shard_map/all_to_all | solution.py:119
  698.9 25.1 %copy-start.2 = (bf16[2048,512]{1,0:T(8,128)(2,1)S(1)}, bf16[2048,512]{1,0:T(8,128)(2,1)}, u32[]{:S(2)}) copy-start(bf16[2048,512]{1,0:T(8,128)(2,1)} %convert_element_type.96) | copy-start | bytes 6291460
  724.0 13.9 %copy-start.1 = (bf16[128,2048]{1,0:T(8,128)(2,1)S(1)}, bf16[128,2048]{1,0:T(8,128)(2,1)}, u32[]{:S(2)}) copy-start(bf16[128,2048]{1,0:T(8,128)(2,1)} %param.3) | copy-start | bytes 1572868
Sparse Core Ops, SparseCore 0:
  44.1 34.2 reduce-scatter.1
where the time goes:
time: 747 us; the launch traced here: 745 us
  waiting for transfers between devices  211 us (28%)
  blocking collectives  195 us (26%)
  other arithmetic  163 us (22%)
  local copies, waits for them, and re-layouts  116 us (16%)
  starting transfers between devices  29.3 us (4%)
  matrix products  17.5 us (2%)
  between operations  13.6 us (2%)
    all_to_all x1, blocking collectives, on_device(): lax.all_to_all(cross_spec, 'fibre', split_axis=0, concat_axis=3, tiled=True)  195 us
    all_to_all x1, waiting for transfers between devices, on_device(): lax.all_to_all(lax.all_to_all(cross_spec, 'fibre', split_axis=0, concat_a...  172 us
    another operation x3, other arithmetic  101 us
    all_to_all x1, local copies, waits for them, and re-layouts, on_device(): lax.all_to_all(lax.all_to_all(cross_spec, 'fibre', split_axis=0, concat_a...  41.3 us
    another operation x1, other arithmetic, one_offset(): return jnp.stack([real_part, imag_part], axis=1).astype(jnp.bfloat16)  40.7 us
    gather x1, local copies, waits for them, and re-layouts, one_offset(): lax.dynamic_slice_in_dim(extended, offset + 1, width, 2).astype(jnp.float32)  36.8 us
    reduce_scatter x1, waiting for transfers between devices, on_device(): lax.psum_scatter(product.reshape(lax.axis_size('band') * local_nf, 2, cha...  34.2 us
    another operation x1, local copies, waits for them, and re-layouts  25.1 us
  transfers between devices with their start and end apart: 5, of which 4 were waited for; matrix products, arithmetic and copies ran while one was open for 2% of the time, Pallas kernels for 0%

commit v1 on v0

v1 whole, which is shorter than its diff:
```python
import math

import jax
import jax.numpy as jnp
import ml_dtypes
import numpy as np
from jax import lax
from jax.experimental import pallas as pl
from jax.experimental.pallas import tpu as pltpu
from jax.sharding import PartitionSpec as P

NT = 8192
NF = 1024
HW = 32
OFFS = 128
LAGS = 512
TURNS = 4
QUART = NT // TURNS
SUB = NF // TURNS
HALF = LAGS // 2
LANE = 128
epsilon = 1e-06
ALL = ("fibre", "band")


def bins():
    return np.arange(TURNS)[:, None] + TURNS * np.arange(SUB)[None, :]


def dft_table():
    phase = np.arange(QUART, dtype=np.int64)[:, None, None] * bins()[None] % NT
    angles = phase * (2.0 * math.pi / NT)
    table = np.stack([np.cos(angles), -np.sin(angles)], axis=2)
    return table.reshape(QUART, 2 * NF).astype(ml_dtypes.bfloat16)


def window_bands():
    gap = np.arange(SUB)[:, None] - np.arange(SUB)[None, :]
    reach = HW // TURNS
    same = np.abs(gap) <= reach
    later = (gap >= -reach) & (gap < reach)
    earlier = (gap > -reach) & (gap <= reach)
    return np.stack([same, later, earlier]).astype(ml_dtypes.bfloat16)


def window_counts():
    k = bins()
    counts = np.minimum(k + HW, NF - 1) - np.maximum(k - HW, 0) + 1
    return (1.0 / counts).astype(np.float32).reshape(TURNS, 1, SUB)


def half_sample():
    angle = bins().reshape(1, NF) * (math.pi / NT)
    return np.stack([np.cos(angle), np.sin(angle)]).astype(np.float32)


def lag_tables():
    k = bins().reshape(NF, 1)
    angle = k * (np.arange(HALF)[None, :] + 0.5) * (2.0 * math.pi / NT)
    weight = np.where(k == 0, 1.0, 2.0) / math.sqrt(NF)
    return np.stack([weight * np.cos(angle), weight * np.sin(angle)]).astype(ml_dtypes.bfloat16)


def flip_matrix():
    return np.eye(HALF)[::-1].astype(ml_dtypes.bfloat16)


def own_column(row, first, rows):
    shape = (rows, row.shape[1])
    lane = lax.broadcasted_iota(jnp.int32, shape, 1)
    line = lax.broadcasted_iota(jnp.int32, shape, 0)
    picked = jnp.where(lane == line + first, jnp.broadcast_to(row, shape), 0.0)
    return jnp.sum(picked, axis=1, keepdims=True)


def bf16_terms(values):
    high = values.astype(jnp.bfloat16)
    rest = values - high.astype(jnp.float32)
    middle = rest.astype(jnp.bfloat16)
    low = (rest - middle.astype(jnp.float32)).astype(jnp.bfloat16)
    return high, middle, low


def exact_dot(values, table):
    total = None
    for term in bf16_terms(values):
        part = jnp.dot(term, table, preferred_element_type=jnp.float32)
        total = part if total is None else total + part
    return total


def whiten_kernel(rank_ref, x_ref, table_ref, bands_ref, counts_ref, alive_ref, out_ref):
    own = x_ref.shape[0] // TURNS
    x = x_ref[...]
    real, imag = [], []
    for m in range(TURNS):
        prod = jnp.dot(
            x, table_ref[:, pl.ds(m * 2 * SUB, 2 * SUB)], preferred_element_type=jnp.float32
        )
        re, im = None, None
        for b in range(TURNS):
            cos_part = prod[b * own : (b + 1) * own, :SUB]
            sin_part = prod[b * own : (b + 1) * own, SUB:]
            turn = b * m % TURNS
            add_re = (cos_part, sin_part, -cos_part, -sin_part)[turn]
            add_im = (sin_part, -cos_part, -sin_part, cos_part)[turn]
            re = add_re if re is None else re + add_re
            im = add_im if im is None else im + add_im
        real.append(re)
        imag.append(im)
    power = [re * re + im * im for re, im in zip(real, imag)]
    alive = own_column(alive_ref[...].astype(jnp.float32), rank_ref[0] * own, own)
    after, before = [None] * TURNS, [None] * TURNS
    for m in range(1, TURNS):
        before[m] = power[m - 1] if m == 1 else before[m - 1] + power[m - 1]
    for m in range(TURNS - 2, -1, -1):
        after[m] = power[m + 1] if m == TURNS - 2 else after[m + 1] + power[m + 1]
    same = exact_dot(jnp.concatenate(power), bands_ref[0])
    later = exact_dot(jnp.concatenate(after[:-1]), bands_ref[1])
    earlier = exact_dot(jnp.concatenate(before[1:]), bands_ref[2])
    for m in range(TURNS):
        total = same[m * own : (m + 1) * own]
        if m < TURNS - 1:
            total = total + later[m * own : (m + 1) * own]
        if m > 0:
            total = total + earlier[(m - 1) * own : m * own]
        scale = alive / jnp.sqrt(total * counts_ref[m] + epsilon)
        out_ref[:, pl.ds(m * SUB, SUB)] = (real[m] * scale).astype(out_ref.dtype)
        out_ref[:, pl.ds(NF + m * SUB, SUB)] = (imag[m] * scale).astype(out_ref.dtype)


def whitened_spectra(rank, x, alive):
    own = x.shape[0] // TURNS
    smem = pl.BlockSpec(memory_space=pltpu.SMEM)
    vmem = pl.BlockSpec(memory_space=pltpu.VMEM)
    return pl.pallas_call(
        whiten_kernel,
        out_shape=jax.ShapeDtypeStruct((own, 2 * NF), jnp.bfloat16),
        in_specs=[smem] + [vmem] * 5,
        out_specs=vmem,
        compiler_params=pltpu.CompilerParams(vmem_limit_bytes=32 << 20),
        name="whiten",
    )(
        rank,
        x,
        jnp.asarray(dft_table()),
        jnp.asarray(window_bands()),
        jnp.asarray(window_counts()),
        alive,
    )


STEP = 16


def lag_kernel(*refs):
    rank_ref, *piece_refs = refs[:6]
    reach_ref, shift_ref, basis_ref, flip_ref, out_ref, a_ref, b_ref, c_ref = refs[6:]
    own = piece_refs[0].shape[0]
    tiles = NF // LANE
    step = pl.program_id(0)

    @pl.when(step == 0)
    def _():
        for p, piece in enumerate(piece_refs):
            for j in range(2 * tiles):
                part = piece[:, pl.ds(j * LANE, LANE)].astype(jnp.float32)
                b_ref[j, pl.ds(p * own, own), :] = part
        for j in range(tiles):
            re = b_ref[j, pl.ds(0, own), :]
            im = b_ref[tiles + j, pl.ds(0, own), :]
            cos = shift_ref[0, :, pl.ds(j * LANE, LANE)]
            sin = shift_ref[1, :, pl.ds(j * LANE, LANE)]
            a_ref[j] = re * cos + im * sin
            a_ref[tiles + j] = im * cos - re * sin

    first = step * STEP
    for j in range(tiles):
        a_re, a_im = a_ref[j], a_ref[tiles + j]
        for i in range(STEP):
            b_re = b_ref[j, pl.ds(first + i + 1, own), :]
            b_im = b_ref[tiles + j, pl.ds(first + i + 1, own), :]
            rows, lanes = pl.ds(i * own, own), pl.ds(j * LANE, LANE)
            c_ref[0, rows, lanes] = (a_re * b_re + a_im * b_im).astype(jnp.bfloat16)
            c_ref[1, rows, lanes] = (a_im * b_re - a_re * b_im).astype(jnp.bfloat16)
    even = jnp.dot(c_ref[0], basis_ref[0], preferred_element_type=jnp.float32)
    odd = jnp.dot(c_ref[1], basis_ref[1], preferred_element_type=jnp.float32)
    reach = own_column(reach_ref[...].astype(jnp.float32), rank_ref[0] * own, own)
    keep = jnp.concatenate([reach >= (first + i + 1).astype(jnp.float32) for i in range(STEP)])
    keep = jnp.broadcast_to(keep, even.shape)
    ahead = jnp.where(keep, even - odd, 0.0).astype(jnp.bfloat16)
    behind = jnp.where(keep, even + odd, 0.0).astype(jnp.bfloat16)
    behind = jnp.dot(behind, flip_ref[...], preferred_element_type=jnp.float32).astype(jnp.bfloat16)
    out_ref[:, :, pl.ds(0, HALF)] = behind.reshape(STEP, own, HALF)
    out_ref[:, :, pl.ds(HALF, HALF)] = ahead.reshape(STEP, own, HALF)


def lag_correlations(rank, pieces, reach):
    own = pieces[0].shape[0]
    vmem = pl.BlockSpec(memory_space=pltpu.VMEM)
    return pl.pallas_call(
        lag_kernel,
        out_shape=jax.ShapeDtypeStruct((OFFS, own, LAGS), jnp.bfloat16),
        grid=(OFFS // STEP,),
        in_specs=[pl.BlockSpec(memory_space=pltpu.SMEM)] + [vmem] * 9,
        out_specs=pl.BlockSpec((STEP, own, LAGS), lambda i: (i, 0, 0)),
        scratch_shapes=[
            pltpu.VMEM((2 * NF // LANE, own, LANE), jnp.float32),
            pltpu.VMEM((2 * NF // LANE, len(pieces) * own, LANE), jnp.float32),
            pltpu.VMEM((2, STEP * own, NF), jnp.bfloat16),
        ],
        compiler_params=pltpu.CompilerParams(vmem_limit_bytes=32 << 20),
        name="lags",
    )(
        rank,
        *pieces,
        reach,
        jnp.asarray(half_sample()),
        jnp.asarray(lag_tables()),
        jnp.asarray(flip_matrix()),
    )


def on_device(traces, alive, reach):
    channels, samples = traces.shape
    bands = lax.axis_size("band")
    count = lax.axis_size("fibre") * bands
    own = channels // bands
    rank = lax.axis_index("band").astype(jnp.int32).reshape(1)
    quarters = lax.all_to_all(
        traces.reshape(bands, own, samples), "band", split_axis=0, concat_axis=0, tiled=True
    )
    whitened = whitened_spectra(
        rank, quarters.reshape(channels, samples), alive.reshape(1, channels)
    )
    pieces = [whitened] + [
        lax.ppermute(whitened, ALL, [(i + j, i) for i in range(count - j)])
        for j in range(1, OFFS // own + 1)
    ]
    lagged = lag_correlations(rank, pieces, reach.reshape(1, channels))
    return lax.all_to_all(lagged, ALL, split_axis=0, concat_axis=1, tiled=True)


def solution(mesh):
    return jax.shard_map(
        on_device,
        mesh=mesh,
        in_specs=(P("fibre", "band"), P("fibre"), P("fibre")),
        out_specs=P(ALL, None, None),
        check_vma=False,
    )
```

time: 747 us -> 117 us (0.16)
  the two profiles are of different devices: /device:TPU:10 before, /device:TPU:0 now
where the time goes in v1:
time: 117 us
  blocking collectives  66.9 us (57%)
  waiting for transfers between devices  17.5 us (15%)
  Pallas kernels  13.9 us (12%)
  starting transfers between devices  10.4 us (9%)
  local copies, waits for them, and re-layouts  7.75 us (7%)
    all_to_all x1, blocking collectives, on_device(): return lax.all_to_all(lagged, ALL, split_axis=0, concat_axis=1, tiled=True)  66.9 us
    pallas_call x1, Pallas kernels, lag_correlations(): pl.pallas_call(lag_kernel, out_shape=jax.ShapeDtypeStruct((OFFS, own, LAG...  12.1 us
    all_to_all x1, waiting for transfers between devices, on_device(): lax.all_to_all(traces.reshape(bands, own, samples), 'band', split_axis=0,...  10.4 us
    unnamed x17, local copies, waits for them, and re-layouts  7.75 us
    ppermute x4, waiting for transfers between devices, on_device(): lax.ppermute(whitened, ALL, [(i + j, i) for i in range(count - j)])  7.12 us
    all_to_all x1, starting transfers between devices, on_device(): lax.all_to_all(traces.reshape(bands, own, samples), 'band', split_axis=0,...  5.23 us
    ppermute x4, starting transfers between devices, on_device(): lax.ppermute(whitened, ALL, [(i + j, i) for i in range(count - j)])  5.17 us
  transfers between devices with their start and end apart: 5, of which 4 were waited for; matrix products, arithmetic and copies ran while one was open for 0% of the time, Pallas kernels for 0%

profile of v1, /device:TPU:0, one launch (start us, length us, event | category | flops | bytes accessed | tf_op | source)
XLA Modules:
  0.0 116.6 jit_solution(9034887974046692561)
XLA Ops:
  0.0 5.2 %all-to-all-start = ((bf16[4,32,2048]{2,1,0:T(8,128)(2,1)}), bf16[4,32,2048]{2,1,0:T(8,128)(2,1)S(1)}, u32[]{:S(2)}, u32[]{:S(2)}) async-start(bf16[4,32,2048]{2,1,0:T(8,128)(2,1)} %bitcast.10), calls=%async_computation | async-start | bytes 1048576 | tf_op jit(solution)/shard_map/all_to_all | solution.py:230
  5.2 10.4 %all-to-all-done = bf16[4,32,2048]{2,1,0:T(8,128)(2,1)S(1)} async-done(((bf16[4,32,2048]{2,1,0:T(8,128)(2,1)}), bf16[4,32,2048]{2,1,0:T(8,128)(2,1)S(1)}, u32[]{:S(2)}, u32[]{:S(2)}) %all-to-all-start) | async-done | bytes 524320 | tf_op jit(solution)/shard_map/all_to_all | solution.py:230
  15.6 0.0 copy-start
  15.6 3.4 %copy-done = bf16[2048,2048]{1,0:T(8,128)(2,1)S(1)} copy-done((bf16[2048,2048]{1,0:T(8,128)(2,1)S(1)}, bf16[2048,2048]{1,0:T(8,128)(2,1)}, u32[]{:S(2)}) %copy-start) | copy-done | bytes 8388632
  19.0 0.0 copy-start.2
  19.0 1.0 copy-done.2
  20.0 0.0 copy-start.5
  20.0 0.7 copy-done.5
  20.6 0.0 copy-start.6
  20.6 0.7 copy-done.6
  21.3 0.0 copy-start.1
  21.3 0.0 copy-start.3
  21.3 0.0 copy-start.4
  21.3 0.0 copy-start.7
  21.3 1.8 %whiten.1.refs_1_ = bf16[32,2048]{1,0:T(8,128)(2,1)S(1)} custom-call(s32[1]{0:T(128)} %bitcast.rank_ref.refs_0_, bf16[128,2048]{1,0:T(8,128)(2,1)S(1)} %bitcast.6, bf16[2048,2048]{1,0:T(8,128)(2,1)S(1)} %copy-done, bf16[3,256,256]{2,1,0:T(8,128)(2,1)S(1)} %copy-done.2, f32[4,1,256]{2,1,0:T(1,128)S(1)} %copy-done.5, s32[1,128]{1,0:T(1,128)S(1)} %bitcast.7), custom_call_target="tpu_custom_call" | custom-call | tf_op jit(solution)/shard_map/whiten/pallas_call | solution.py:136
  23.2 1.3 %collective-permute-start.3 = (bf16[32,2048]{1,0:T(8,128)(2,1)S(1)}, bf16[32,2048]{1,0:T(8,128)(2,1)S(1)}, u32[]{:S(2)}, u32[]{:S(2)}) collective-permute-start(bf16[32,2048]{1,0:T(8,128)(2,1)S(1)} %whiten.1.refs_1_), channel_id=1, source_target_pairs={{4,0},{5,1},{6,2},{7,3},{8,4},{9,5},{10,6},{11,7},{12,8},{13,9},{1... | collective-permute-start | bytes 393224 | tf_op jit(solution)/shard_map/ppermute | solution.py:237
  24.5 1.3 %collective-permute-start.2 = (bf16[32,2048]{1,0:T(8,128)(2,1)S(1)}, bf16[32,2048]{1,0:T(8,128)(2,1)S(1)}, u32[]{:S(2)}, u32[]{:S(2)}) collective-permute-start(bf16[32,2048]{1,0:T(8,128)(2,1)S(1)} %whiten.1.refs_1_), channel_id=1, source_target_pairs={{3,0},{4,1},{5,2},{6,3},{7,4},{8,5},{9,6},{10,7},{11,8},{12,9},{13... | collective-permute-start | bytes 393224 | tf_op jit(solution)/shard_map/ppermute | solution.py:237
  25.8 1.3 %collective-permute-start.1 = (bf16[32,2048]{1,0:T(8,128)(2,1)S(1)}, bf16[32,2048]{1,0:T(8,128)(2,1)S(1)}, u32[]{:S(2)}, u32[]{:S(2)}) collective-permute-start(bf16[32,2048]{1,0:T(8,128)(2,1)S(1)} %whiten.1.refs_1_), channel_id=1, source_target_pairs={{2,0},{3,1},{4,2},{5,3},{6,4},{7,5},{8,6},{9,7},{10,8},{11,9},{12,... | collective-permute-start | bytes 393224 | tf_op jit(solution)/shard_map/ppermute | solution.py:237
  27.1 1.3 %collective-permute-start = (bf16[32,2048]{1,0:T(8,128)(2,1)S(1)}, bf16[32,2048]{1,0:T(8,128)(2,1)S(1)}, u32[]{:S(2)}, u32[]{:S(2)}) collective-permute-start(bf16[32,2048]{1,0:T(8,128)(2,1)S(1)} %whiten.1.refs_1_), channel_id=1, source_target_pairs={{1,0},{2,1},{3,2},{4,3},{5,4},{6,5},{7,6},{8,7},{9,8},{10,9},{11,1... | collective-permute-start | bytes 393224 | tf_op jit(solution)/shard_map/ppermute | solution.py:237
  28.4 2.7 %collective-permute-done.3.refs_5_ = bf16[32,2048]{1,0:T(8,128)(2,1)S(1)} collective-permute-done((bf16[32,2048]{1,0:T(8,128)(2,1)S(1)}, bf16[32,2048]{1,0:T(8,128)(2,1)S(1)}, u32[]{:S(2)}, u32[]{:S(2)}) %collective-permute-start.3) | collective-permute-done | bytes 131104 | tf_op jit(solution)/shard_map/ppermute | solution.py:237
  31.0 1.2 %collective-permute-done.2.refs_4_ = bf16[32,2048]{1,0:T(8,128)(2,1)S(1)} collective-permute-done((bf16[32,2048]{1,0:T(8,128)(2,1)S(1)}, bf16[32,2048]{1,0:T(8,128)(2,1)S(1)}, u32[]{:S(2)}, u32[]{:S(2)}) %collective-permute-start.2) | collective-permute-done | bytes 131104 | tf_op jit(solution)/shard_map/ppermute | solution.py:237
  32.3 3.2 %collective-permute-done.1.refs_3_ = bf16[32,2048]{1,0:T(8,128)(2,1)S(1)} collective-permute-done((bf16[32,2048]{1,0:T(8,128)(2,1)S(1)}, bf16[32,2048]{1,0:T(8,128)(2,1)S(1)}, u32[]{:S(2)}, u32[]{:S(2)}) %collective-permute-start.1) | collective-permute-done | bytes 131104 | tf_op jit(solution)/shard_map/ppermute | solution.py:237
  35.5 0.0 collective-permute-done.refs_2_
  35.5 0.0 copy-done.1
  35.5 0.0 copy-done.3
  35.5 0.0 copy-done.4
  35.5 0.0 copy-done.7
  35.5 12.1 %lags.1 = bf16[128,32,512]{2,1,0:T(8,128)(2,1)S(1)} custom-call(s32[1]{0:T(128)} %bitcast.rank_ref.refs_0_, bf16[32,2048]{1,0:T(8,128)(2,1)S(1)} %whiten.1.refs_1_, bf16[32,2048]{1,0:T(8,128)(2,1)S(1)} %collective-permute-done.refs_2_, bf16[32,2048]{1,0:T(8,128)(2,1)S(1)} %collective-permute-done.1.refs_3_, ...), custom_call_target="tpu_custom_call" | custom-call | tf_op jit(solution)/shard_map/lags/pallas_call | solution.py:201
  47.6 66.9 %all_to_all.17 = bf16[128,32,512]{2,1,0:T(8,128)(2,1)S(1)} all-to-all(bf16[128,32,512]{2,1,0:T(8,128)(2,1)S(1)} %lags.1), channel_id=1, replica_groups=mesh['fibre'=32,'band'=4] {'fibre','band'}, dimensions={0} | all-to-all | bytes 8388608 | tf_op jit(solution)/shard_map/all_to_all | solution.py:241
  114.5 2.0 %copy.11 = bf16[1,4096,512]{2,1,0:T(8,128)(2,1)} copy(bf16[1,4096,512]{2,1,0:T(8,128)(2,1)S(1)} %bitcast.9) | data formatting | bytes 8388608
Async XLA Ops:
  0.0 15.6 %all-to-all-start = ((bf16[4,32,2048]{2,1,0:T(8,128)(2,1)}), bf16[4,32,2048]{2,1,0:T(8,128)(2,1)S(1)}, u32[]{:S(2)}, u32[]{:S(2)}) async-start(bf16[4,32,2048]{2,1,0:T(8,128)(2,1)} %bitcast.10), calls=%async_computation | async-start | bytes 1048576 | tf_op jit(solution)/shard_map/all_to_all | solution.py:230
  15.6 3.4 %copy-start = (bf16[2048,2048]{1,0:T(8,128)(2,1)S(1)}, bf16[2048,2048]{1,0:T(8,128)(2,1)}, u32[]{:S(2)}) copy-start(bf16[2048,2048]{1,0:T(8,128)(2,1)} %constant.16.clone.table_ref) | copy-start | bytes 25165828
  19.0 1.0 copy-start.2
  20.0 0.7 copy-start.5
  20.6 0.7 copy-start.6
  21.3 14.2 %copy-start.1 = (bf16[2,1024,256]{2,1,0:T(8,128)(2,1)S(1)}, bf16[2,1024,256]{2,1,0:T(8,128)(2,1)}, u32[]{:S(2)}) copy-start(bf16[2,1024,256]{2,1,0:T(8,128)(2,1)} %constant.20.clone.refs_8_) | copy-start | bytes 3145732
  21.3 14.2 %copy-start.3 = (bf16[256,256]{1,0:T(8,128)(2,1)S(1)}, bf16[256,256]{1,0:T(8,128)(2,1)}, u32[]{:S(2)}) copy-start(bf16[256,256]{1,0:T(8,128)(2,1)} %constant.21.clone.refs_9_) | copy-start | bytes 393220
  21.3 14.2 %copy-start.4 = (f32[2,1,1024]{2,1,0:T(1,128)S(1)}, f32[2,1,1024]{2,1,0:T(1,128)}, u32[]{:S(2)}) copy-start(f32[2,1,1024]{2,1,0:T(1,128)} %constant.19.clone.refs_7_) | copy-start | bytes 24580
  21.3 14.2 %copy-start.7 = (s32[128]{0:T(128)S(1)}, s32[128]{0:T(128)}, u32[]{:S(2)}) copy-start(s32[128]{0:T(128)} %param.11) | copy-start | bytes 1540
  23.2 7.9 %collective-permute-start.3 = (bf16[32,2048]{1,0:T(8,128)(2,1)S(1)}, bf16[32,2048]{1,0:T(8,128)(2,1)S(1)}, u32[]{:S(2)}, u32[]{:S(2)}) collective-permute-start(bf16[32,2048]{1,0:T(8,128)(2,1)S(1)} %whiten.1.refs_1_), channel_id=1, source_target_pairs={{4,0},{5,1},{6,2},{7,3},{8,4},{9,5},{10,6},{11,7},{12,8},{13,9},{1... | collective-permute-start | bytes 393224 | tf_op jit(solution)/shard_map/ppermute | solution.py:237
  24.5 7.8 %collective-permute-start.2 = (bf16[32,2048]{1,0:T(8,128)(2,1)S(1)}, bf16[32,2048]{1,0:T(8,128)(2,1)S(1)}, u32[]{:S(2)}, u32[]{:S(2)}) collective-permute-start(bf16[32,2048]{1,0:T(8,128)(2,1)S(1)} %whiten.1.refs_1_), channel_id=1, source_target_pairs={{3,0},{4,1},{5,2},{6,3},{7,4},{8,5},{9,6},{10,7},{11,8},{12,9},{13... | collective-permute-start | bytes 393224 | tf_op jit(solution)/shard_map/ppermute | solution.py:237
  25.8 9.7 %collective-permute-start.1 = (bf16[32,2048]{1,0:T(8,128)(2,1)S(1)}, bf16[32,2048]{1,0:T(8,128)(2,1)S(1)}, u32[]{:S(2)}, u32[]{:S(2)}) collective-permute-start(bf16[32,2048]{1,0:T(8,128)(2,1)S(1)} %whiten.1.refs_1_), channel_id=1, source_target_pairs={{2,0},{3,1},{4,2},{5,3},{6,4},{7,5},{8,6},{9,7},{10,8},{11,9},{12,... | collective-permute-start | bytes 393224 | tf_op jit(solution)/shard_map/ppermute | solution.py:237
  27.1 8.4 %collective-permute-start = (bf16[32,2048]{1,0:T(8,128)(2,1)S(1)}, bf16[32,2048]{1,0:T(8,128)(2,1)S(1)}, u32[]{:S(2)}, u32[]{:S(2)}) collective-permute-start(bf16[32,2048]{1,0:T(8,128)(2,1)S(1)} %whiten.1.refs_1_), channel_id=1, source_target_pairs={{1,0},{2,1},{3,2},{4,3},{5,4},{6,5},{7,6},{8,7},{9,8},{10,9},{11,1... | collective-permute-start | bytes 393224 | tf_op jit(solution)/shard_map/ppermute | solution.py:237

commit v2 on v1

--- a/solution.py
+++ b/solution.py
@@ -17,8 +17,10 @@
 TURNS = 4
 QUART = NT // TURNS
 SUB = NF // TURNS
-HALF = LAGS // 2
 LANE = 128
+COEFS = 160
+GROUPS = LANE // (COEFS - LANE)
+CORES = 2
 epsilon = 1e-06
 ALL = ("fibre", "band")
 
@@ -49,20 +51,29 @@
     return (1.0 / counts).astype(np.float32).reshape(TURNS, 1, SUB)
 
 
-def half_sample():
-    angle = bins().reshape(1, NF) * (math.pi / NT)
-    return np.stack([np.cos(angle), np.sin(angle)]).astype(np.float32)
+def lag_vectors():
+    n = np.arange(LAGS)
+    width = NF / NT
+    diagonal = ((LAGS - 1 - 2 * n) / 2.0) ** 2 * math.cos(2 * math.pi * width)
+    beside = n[1:] * (LAGS - n[1:]) / 2.0
+    matrix = np.diag(diagonal) + np.diag(beside, 1) + np.diag(beside, -1)
+    vectors = np.linalg.eigh(matrix)[1][:, ::-1][:, :COEFS].T
+    return vectors * np.where(vectors[:, LAGS // 2] < 0, -1.0, 1.0)[:, None]
+
+
+def repeated(table):
+    return np.concatenate([table[:, :LANE]] + [table[:, LANE:]] * GROUPS, axis=1)
 
 
 def lag_tables():
     k = bins().reshape(NF, 1)
-    angle = k * (np.arange(HALF)[None, :] + 0.5) * (2.0 * math.pi / NT)
+    angle = k * (np.arange(LAGS)[None, :] - LAGS // 2) * (2.0 * math.pi / NT)
     weight = np.where(k == 0, 1.0, 2.0) / math.sqrt(NF)
-    return np.stack([weight * np.cos(angle), weight * np.sin(angle)]).astype(ml_dtypes.bfloat16)
-
-
-def flip_matrix():
-    return np.eye(HALF)[::-1].astype(ml_dtypes.bfloat16)
+    table = np.concatenate([weight * np.cos(angle), -weight * np.sin(angle)])
+    vectors = lag_vectors()
+    project = repeated(table @ vectors.T)
+    expand = repeated(vectors.T).T
+    return project.astype(ml_dtypes.bfloat16), expand.astype(ml_dtypes.bfloat16)
 
 
 def own_column(row, first, rows):
@@ -150,75 +161,107 @@
     )
 
 
-STEP = 16
-
-
-def lag_kernel(*refs):
-    rank_ref, *piece_refs = refs[:6]
-    reach_ref, shift_ref, basis_ref, flip_ref, out_ref, a_ref, b_ref, c_ref = refs[6:]
+STEP = 8
+
+
+def group_mask(rows):
+    lane = lax.broadcasted_iota(jnp.int32, (rows, LANE), 1)
+    line = lax.broadcasted_iota(jnp.int32, (rows, LANE), 0)
+    return lane // (LANE // GROUPS) == line // (rows // GROUPS)
+
+
+def lag_kernel(rank_ref, *refs):
+    piece_refs, reach_ref, table_ref, out_ref, b_ref, c_ref = refs[:-5], *refs[-5:]
+    blocks = len(piece_refs) // CORES
     own = piece_refs[0].shape[0]
-    tiles = NF // LANE
+    rows = CORES * own
+    tiles = 2 * NF // LANE
     step = pl.program_id(0)
+    core = rank_ref[0] % CORES
 
     @pl.when(step == 0)
     def _():
-        for p, piece in enumerate(piece_refs):
-            for j in range(2 * tiles):
-                part = piece[:, pl.ds(j * LANE, LANE)].astype(jnp.float32)
-                b_ref[j, pl.ds(p * own, own), :] = part
-        for j in range(tiles):
-            re = b_ref[j, pl.ds(0, own), :]
-            im = b_ref[tiles + j, pl.ds(0, own), :]
-            cos = shift_ref[0, :, pl.ds(j * LANE, LANE)]
-            sin = shift_ref[1, :, pl.ds(j * LANE, LANE)]
-            a_ref[j] = re * cos + im * sin
-            a_ref[tiles + j] = im * cos - re * sin
-
-    first = step * STEP
-    for j in range(tiles):
-        a_re, a_im = a_ref[j], a_ref[tiles + j]
+        for p in range(blocks):
+            for swap in range(CORES):
+                at = p * rows + own * (core + swap - 2 * core * swap)
+                for j in range(tiles):
+                    part = piece_refs[CORES * p + swap][:, pl.ds(j * LANE, LANE)]
+                    b_ref[j, pl.ds(pl.multiple_of(at, own), own), :] = part.astype(jnp.float32)
+
+    first = CORES * STEP * step + core + 1
+    for j in range(tiles // 2):
+        a_re, a_im = b_ref[j, pl.ds(0, rows), :], b_ref[tiles // 2 + j, pl.ds(0, rows), :]
         for i in range(STEP):
-            b_re = b_ref[j, pl.ds(first + i + 1, own), :]
-            b_im = b_ref[tiles + j, pl.ds(first + i + 1, own), :]
-            rows, lanes = pl.ds(i * own, own), pl.ds(j * LANE, LANE)
-            c_ref[0, rows, lanes] = (a_re * b_re + a_im * b_im).astype(jnp.bfloat16)
-            c_ref[1, rows, lanes] = (a_im * b_re - a_re * b_im).astype(jnp.bfloat16)
-    even = jnp.dot(c_ref[0], basis_ref[0], preferred_element_type=jnp.float32)
-    odd = jnp.dot(c_ref[1], basis_ref[1], preferred_element_type=jnp.float32)
-    reach = own_column(reach_ref[...].astype(jnp.float32), rank_ref[0] * own, own)
-    keep = jnp.concatenate([reach >= (first + i + 1).astype(jnp.float32) for i in range(STEP)])
-    keep = jnp.broadcast_to(keep, even.shape)
-    ahead = jnp.where(keep, even - odd, 0.0).astype(jnp.bfloat16)
-    behind = jnp.where(keep, even + odd, 0.0).astype(jnp.bfloat16)
-    behind = jnp.dot(behind, flip_ref[...], preferred_element_type=jnp.float32).astype(jnp.bfloat16)
-    out_ref[:, :, pl.ds(0, HALF)] = behind.reshape(STEP, own, HALF)
-    out_ref[:, :, pl.ds(HALF, HALF)] = ahead.reshape(STEP, own, HALF)
-
-
-def lag_correlations(rank, pieces, reach):
+            near = pl.ds(first + CORES * i, rows)
+            b_re, b_im = b_ref[j, near, :], b_ref[tiles // 2 + j, near, :]
+            line = pl.ds(i * rows, rows)
+            c_ref[line, pl.ds(j * LANE, LANE)] = (a_re * b_re + a_im * b_im).astype(jnp.bfloat16)
+            c_ref[line, pl.ds(NF + j * LANE, LANE)] = (a_im * b_re - a_re * b_im).astype(
+                jnp.bfloat16
+            )
+    coefs = jnp.dot(c_ref[...], table_ref[...], preferred_element_type=jnp.float32)
+    reach = own_column(
+        reach_ref[...].astype(jnp.float32), rank_ref[0] // CORES * rows, rows
+    )
+    member = group_mask(rows)
+    for i in range(STEP):
+        part = coefs[i * rows : (i + 1) * rows]
+        keep = jnp.broadcast_to(reach, (rows, LANE)) >= (first + CORES * i).astype(jnp.float32)
+        out_ref[i, pl.ds(0, rows), :] = jnp.where(keep, part[:, :LANE], 0.0).astype(jnp.bfloat16)
+        rest = jnp.where(keep & member, part[:, LANE:], 0.0)
+        rest = jnp.sum(rest.reshape(GROUPS, rows // GROUPS, LANE), axis=0)
+        out_ref[i, pl.ds(rows, rows // GROUPS), :] = rest.astype(jnp.bfloat16)
+
+
+def lag_coefficients(rank, pieces, reach, table):
     own = pieces[0].shape[0]
+    rows = CORES * own
+    offsets = OFFS // CORES
+    packed = rows + rows // GROUPS
     vmem = pl.BlockSpec(memory_space=pltpu.VMEM)
     return pl.pallas_call(
         lag_kernel,
-        out_shape=jax.ShapeDtypeStruct((OFFS, own, LAGS), jnp.bfloat16),
-        grid=(OFFS // STEP,),
-        in_specs=[pl.BlockSpec(memory_space=pltpu.SMEM)] + [vmem] * 9,
-        out_specs=pl.BlockSpec((STEP, own, LAGS), lambda i: (i, 0, 0)),
+        out_shape=jax.ShapeDtypeStruct((offsets, packed, LANE), jnp.bfloat16),
+        grid=(offsets // STEP,),
+        in_specs=[pl.BlockSpec(memory_space=pltpu.SMEM)] + [vmem] * (len(pieces) + 2),
+        out_specs=pl.BlockSpec((STEP, packed, LANE), lambda i: (i, 0, 0)),
         scratch_shapes=[
-            pltpu.VMEM((2 * NF // LANE, own, LANE), jnp.float32),
             pltpu.VMEM((2 * NF // LANE, len(pieces) * own, LANE), jnp.float32),
-            pltpu.VMEM((2, STEP * own, NF), jnp.bfloat16),
+            pltpu.VMEM((STEP * rows, 2 * NF), jnp.bfloat16),
         ],
         compiler_params=pltpu.CompilerParams(vmem_limit_bytes=32 << 20),
         name="lags",
-    )(
-        rank,
-        *pieces,
-        reach,
-        jnp.asarray(half_sample()),
-        jnp.asarray(lag_tables()),
-        jnp.asarray(flip_matrix()),
-    )
+    )(rank, *pieces, reach, table)
+
+
+def expand_kernel(coefs_ref, table_ref, out_ref):
+    count, packed, _ = coefs_ref.shape
+    rows = packed * GROUPS // (GROUPS + 1)
+    member = group_mask(rows)
+    lines = []
+    for i in range(count):
+        rest = coefs_ref[i, pl.ds(rows, rows // GROUPS), :].astype(jnp.float32)
+        rest = jnp.where(member, jnp.concatenate([rest] * GROUPS), 0.0).astype(jnp.bfloat16)
+        lines.append(jnp.concatenate([coefs_ref[i, pl.ds(0, rows), :], rest], axis=1))
+    lags = jnp.dot(jnp.concatenate(lines), table_ref[...], preferred_element_type=jnp.float32)
+    out_ref[0] = lags.astype(out_ref.dtype)
+
+
+def expanded(coefs, table):
+    count, packed, _ = coefs.shape
+    rows = packed * GROUPS // (GROUPS + 1)
+    return pl.pallas_call(
+        expand_kernel,
+        out_shape=jax.ShapeDtypeStruct((1, count * rows, LAGS), jnp.bfloat16),
+        grid=(count // STEP,),
+        in_specs=[
+            pl.BlockSpec((STEP, packed, LANE), lambda i: (i, 0, 0)),
+            pl.BlockSpec(memory_space=pltpu.VMEM),
+        ],
+        out_specs=pl.BlockSpec((1, STEP * rows, LAGS), lambda i: (0, i, 0)),
+        compiler_params=pltpu.CompilerParams(vmem_limit_bytes=32 << 20),
+        name="expand",
+    )(coefs, table)
 
 
 def on_device(traces, alive, reach):
@@ -227,18 +270,25 @@
     count = lax.axis_size("fibre") * bands
     own = channels // bands
     rank = lax.axis_index("band").astype(jnp.int32).reshape(1)
+    project, expand = lag_tables()
     quarters = lax.all_to_all(
         traces.reshape(bands, own, samples), "band", split_axis=0, concat_axis=0, tiled=True
     )
     whitened = whitened_spectra(
         rank, quarters.reshape(channels, samples), alive.reshape(1, channels)
     )
-    pieces = [whitened] + [
-        lax.ppermute(whitened, ALL, [(i + j, i) for i in range(count - j)])
-        for j in range(1, OFFS // own + 1)
-    ]
-    lagged = lag_correlations(rank, pieces, reach.reshape(1, channels))
-    return lax.all_to_all(lagged, ALL, split_axis=0, concat_axis=1, tiled=True)
+    pieces = []
+    for chips in range(OFFS // (CORES * own) + 1):
+        by = CORES * chips
+        pairs = [(i + by, i) for i in range(count - by)]
+        piece = lax.ppermute(whitened, ALL, pairs) if by else whitened
+        pieces += [piece, lax.ppermute(piece, ALL, [(i ^ 1, i) for i in range(count)])]
+    coefs = lag_coefficients(rank, pieces, reach.reshape(1, channels), jnp.asarray(project))
+    groups = [list(range(core, count, CORES)) for core in range(CORES)]
+    coefs = lax.all_to_all(
+        coefs, ALL, split_axis=0, concat_axis=0, axis_index_groups=groups, tiled=True
+    )
+    return expanded(coefs, jnp.asarray(expand))
 
 
 def solution(mesh):

time: 117 us -> 82.7 us (0.71)
  blocking collectives: 66.9 us -> 34 us
  starting transfers between devices: 10.4 us -> 8.03 us
  local copies, waits for them, and re-layouts: 7.75 us -> 5.73 us
  Pallas kernels: 13.9 us -> 15.8 us
  waiting for transfers between devices: 17.5 us -> 18.7 us
    all_to_all x1, blocking collectives: 66.9 us -> 34 us  [on_device(): lax.all_to_all(coefs, ALL, split_axis=0, concat_axis=0, axis_index_groups...]
    ppermute x4 -> x5, starting transfers between devices: 5.17 us -> 2.81 us  [the longest x2 2.72 us: on_device(): piece = lax.ppermute(whitened, ALL, pairs) if by else whitened]
    unnamed x17 -> x14, local copies, waits for them, and re-layouts: 7.75 us -> 5.73 us
    pallas_call x1 -> x2, Pallas kernels: 12.1 us -> 14 us  [the longest x1 9.31 us: lag_coefficients(): pl.pallas_call(lag_kernel, out_shape=jax.ShapeDtypeStruct((offsets, packe...]
    ppermute x4 -> x5, waiting for transfers between devices: 7.12 us -> 8.39 us  [the longest x2 7.05 us: on_device(): piece = lax.ppermute(whitened, ALL, pairs) if by else whitened]
  transfers between devices with their start and end apart: 5 -> 6, of which waited for: 4 -> 4; matrix products, arithmetic and copies ran while one was open for 0% -> 0% of each run, Pallas kernels for 0% -> 0%
where the time goes in v2:
time: 82.7 us; the launch traced here: 82.3 us
  blocking collectives  34 us (41%)
  waiting for transfers between devices  18.7 us (23%)
  Pallas kernels  15.8 us (19%)
  starting transfers between devices  8.03 us (10%)
  local copies, waits for them, and re-layouts  5.73 us (7%)
    all_to_all x1, blocking collectives, on_device(): lax.all_to_all(coefs, ALL, split_axis=0, concat_axis=0, axis_index_groups...  34 us
    all_to_all x1, waiting for transfers between devices, on_device(): lax.all_to_all(traces.reshape(bands, own, samples), 'band', split_axis=0,...  10.4 us
    pallas_call x1, Pallas kernels, lag_coefficients(): pl.pallas_call(lag_kernel, out_shape=jax.ShapeDtypeStruct((offsets, packe...  9.31 us
    ppermute x2, waiting for transfers between devices, on_device(): piece = lax.ppermute(whitened, ALL, pairs) if by else whitened  7.05 us
    unnamed x14, local copies, waits for them, and re-layouts  5.73 us
    all_to_all x1, starting transfers between devices, on_device(): lax.all_to_all(traces.reshape(bands, own, samples), 'band', split_axis=0,...  5.23 us
    pallas_call x1, Pallas kernels, expanded(): pl.pallas_call(expand_kernel, out_shape=jax.ShapeDtypeStruct((1, count *...  4.66 us
    ppermute x2, starting transfers between devices, on_device(): piece = lax.ppermute(whitened, ALL, pairs) if by else whitened  2.72 us
  transfers between devices with their start and end apart: 6, of which 4 were waited for; matrix products, arithmetic and copies ran while one was open for 0% of the time, Pallas kernels for 0%

profile of v2, /device:TPU:0, one launch (start us, length us, event | category | flops | bytes accessed | tf_op | source)
XLA Modules:
  0.0 82.3 jit_solution(8198526268495950706)
XLA Ops:
  0.0 5.2 %all-to-all-start = ((bf16[4,32,2048]{2,1,0:T(8,128)(2,1)}), bf16[4,32,2048]{2,1,0:T(8,128)(2,1)S(1)}, u32[]{:S(2)}, u32[]{:S(2)}) async-start(bf16[4,32,2048]{2,1,0:T(8,128)(2,1)} %bitcast.8), calls=%async_computation | async-start | bytes 1048576 | tf_op jit(solution)/shard_map/all_to_all | solution.py:274
  5.2 10.4 %all-to-all-done = bf16[4,32,2048]{2,1,0:T(8,128)(2,1)S(1)} async-done(((bf16[4,32,2048]{2,1,0:T(8,128)(2,1)}), bf16[4,32,2048]{2,1,0:T(8,128)(2,1)S(1)}, u32[]{:S(2)}, u32[]{:S(2)}) %all-to-all-start) | async-done | bytes 524320 | tf_op jit(solution)/shard_map/all_to_all | solution.py:274
  15.6 0.0 copy-start
  15.6 3.4 %copy-done = bf16[2048,2048]{1,0:T(8,128)(2,1)S(1)} copy-done((bf16[2048,2048]{1,0:T(8,128)(2,1)S(1)}, bf16[2048,2048]{1,0:T(8,128)(2,1)}, u32[]{:S(2)}) %copy-start) | copy-done | bytes 8388632
  19.0 0.0 copy-start.2
  19.0 1.0 %copy-done.2 = bf16[3,256,256]{2,1,0:T(8,128)(2,1)S(1)} copy-done((bf16[3,256,256]{2,1,0:T(8,128)(2,1)S(1)}, bf16[3,256,256]{2,1,0:T(8,128)(2,1)}, u32[]{:S(2)}) %copy-start.2) | copy-done | bytes 393240
  20.0 0.0 copy-start.4
  20.0 0.7 copy-done.4
  20.6 0.0 copy-start.5
  20.6 0.7 copy-done.5
  21.3 0.0 copy-start.1
  21.3 0.0 copy-start.6
  21.3 1.8 %whiten.1.refs_0_ = bf16[32,2048]{1,0:T(8,128)(2,1)S(1)} custom-call(s32[1]{0:T(128)} %bitcast.rank_ref, bf16[128,2048]{1,0:T(8,128)(2,1)S(1)} %bitcast.5, bf16[2048,2048]{1,0:T(8,128)(2,1)S(1)} %copy-done, bf16[3,256,256]{2,1,0:T(8,128)(2,1)S(1)} %copy-done.2, f32[4,1,256]{2,1,0:T(1,128)S(1)} %copy-done.4, s32[1,128]{1,0:T(1,128)S(1)} %bitcast.6), custom_call_target="tpu_custom_call" | custom-call | tf_op jit(solution)/shard_map/whiten/pallas_call | solution.py:147
  23.1 0.0 copy-start.3
  23.2 1.4 %collective-permute-start.3 = (bf16[32,2048]{1,0:T(8,128)(2,1)S(1)}, bf16[32,2048]{1,0:T(8,128)(2,1)S(1)}, u32[]{:S(2)}, u32[]{:S(2)}) collective-permute-start(bf16[32,2048]{1,0:T(8,128)(2,1)S(1)} %whiten.1.refs_0_), channel_id=1, source_target_pairs={{4,0},{5,1},{6,2},{7,3},{8,4},{9,5},{10,6},{11,7},{12,8},{13,9},{1... | collective-permute-start | bytes 393224 | tf_op jit(solution)/shard_map/ppermute | solution.py:284
  24.6 1.3 %collective-permute-start.1 = (bf16[32,2048]{1,0:T(8,128)(2,1)S(1)}, bf16[32,2048]{1,0:T(8,128)(2,1)S(1)}, u32[]{:S(2)}, u32[]{:S(2)}) collective-permute-start(bf16[32,2048]{1,0:T(8,128)(2,1)S(1)} %whiten.1.refs_0_), channel_id=1, source_target_pairs={{2,0},{3,1},{4,2},{5,3},{6,4},{7,5},{8,6},{9,7},{10,8},{11,9},{12,... | collective-permute-start | bytes 393224 | tf_op jit(solution)/shard_map/ppermute | solution.py:284
  25.9 0.1 collective-permute-start
  26.0 5.2 %collective-permute-done.3.refs_4_ = bf16[32,2048]{1,0:T(8,128)(2,1)S(1)} collective-permute-done((bf16[32,2048]{1,0:T(8,128)(2,1)S(1)}, bf16[32,2048]{1,0:T(8,128)(2,1)S(1)}, u32[]{:S(2)}, u32[]{:S(2)}) %collective-permute-start.3) | collective-permute-done | bytes 131104 | tf_op jit(solution)/shard_map/ppermute | solution.py:284
  31.2 0.0 collective-permute-start.4
  31.2 1.9 %collective-permute-done.1.refs_2_ = bf16[32,2048]{1,0:T(8,128)(2,1)S(1)} collective-permute-done((bf16[32,2048]{1,0:T(8,128)(2,1)S(1)}, bf16[32,2048]{1,0:T(8,128)(2,1)S(1)}, u32[]{:S(2)}, u32[]{:S(2)}) %collective-permute-start.1) | collective-permute-done | bytes 131104 | tf_op jit(solution)/shard_map/ppermute | solution.py:284
  33.0 0.0 collective-permute-start.2
  33.0 0.0 collective-permute-done.refs_1_
  33.0 0.0 collective-permute-done.4.refs_5_
  33.0 1.3 %collective-permute-done.2.refs_3_ = bf16[32,2048]{1,0:T(8,128)(2,1)S(1)} collective-permute-done((bf16[32,2048]{1,0:T(8,128)(2,1)S(1)}, bf16[32,2048]{1,0:T(8,128)(2,1)S(1)}, u32[]{:S(2)}, u32[]{:S(2)}) %collective-permute-start.2) | collective-permute-done | bytes 131104 | tf_op jit(solution)/shard_map/ppermute | solution.py:285
  34.4 0.0 copy-done.1
  34.4 0.0 copy-done.6
  34.4 9.3 %lags.1 = bf16[64,80,128]{2,1,0:T(8,128)(2,1)S(1)} custom-call(s32[1]{0:T(128)} %bitcast.rank_ref, bf16[32,2048]{1,0:T(8,128)(2,1)S(1)} %whiten.1.refs_0_, bf16[32,2048]{1,0:T(8,128)(2,1)S(1)} %collective-permute-done.refs_1_, bf16[32,2048]{1,0:T(8,128)(2,1)S(1)} %collective-permute-done.1.refs_2_, bf16[32,2048]{1,0:T(8,128)(2,1)S(1)} %collective-permute-done.2.refs_3_, ...), custom_call_target="tpu_custom_call" | custom-call | tf_op jit(solution)/shard_map/lags/pallas_call | solution.py:222
  43.7 34.0 %all_to_all.10.coefs_ref = bf16[64,80,128]{2,1,0:T(8,128)(2,1)S(1)} all-to-all(bf16[64,80,128]{2,1,0:T(8,128)(2,1)S(1)} %lags.1), channel_id=1, replica_groups={{0,2,4,6,8,10,12,14,16,18,20,22,24,26,28,30,32,34,36,38,40,42,44,46,48,..., dimensions={0} | all-to-all | bytes 2621440 | tf_op jit(solution)/shard_map/all_to_all | solution.py:288
  77.7 0.0 copy-done.3
  77.7 4.7 %expand.1 = bf16[1,4096,512]{2,1,0:T(8,128)(2,1)} custom-call(bf16[64,80,128]{2,1,0:T(8,128)(2,1)S(1)} %all_to_all.10.coefs_ref, bf16[256,512]{1,0:T(8,128)(2,1)S(1)} %copy-done.3), custom_call_target="tpu_custom_call" | custom-call | tf_op jit(solution)/shard_map/expand/pallas_call | solution.py:253
Async XLA Ops:
  0.0 15.6 %all-to-all-start = ((bf16[4,32,2048]{2,1,0:T(8,128)(2,1)}), bf16[4,32,2048]{2,1,0:T(8,128)(2,1)S(1)}, u32[]{:S(2)}, u32[]{:S(2)}) async-start(bf16[4,32,2048]{2,1,0:T(8,128)(2,1)} %bitcast.8), calls=%async_computation | async-start | bytes 1048576 | tf_op jit(solution)/shard_map/all_to_all | solution.py:274
  15.6 3.4 %copy-start = (bf16[2048,2048]{1,0:T(8,128)(2,1)S(1)}, bf16[2048,2048]{1,0:T(8,128)(2,1)}, u32[]{:S(2)}) copy-start(bf16[2048,2048]{1,0:T(8,128)(2,1)} %constant.14.clone.table_ref) | copy-start | bytes 25165828
  19.0 1.0 %copy-start.2 = (bf16[3,256,256]{2,1,0:T(8,128)(2,1)S(1)}, bf16[3,256,256]{2,1,0:T(8,128)(2,1)}, u32[]{:S(2)}) copy-start(bf16[3,256,256]{2,1,0:T(8,128)(2,1)} %constant.15.clone.bands_ref) | copy-start | bytes 1179652
  20.0 0.7 copy-start.4
  20.6 0.7 copy-start.5
  21.3 13.1 %copy-start.1 = (bf16[2048,256]{1,0:T(8,128)(2,1)S(1)}, bf16[2048,256]{1,0:T(8,128)(2,1)}, u32[]{:S(2)}) copy-start(bf16[2048,256]{1,0:T(8,128)(2,1)} %constant.17.clone.refs_7_) | copy-start | bytes 3145732
  21.3 13.1 %copy-start.6 = (s32[128]{0:T(128)S(1)}, s32[128]{0:T(128)}, u32[]{:S(2)}) copy-start(s32[128]{0:T(128)} %param.10) | copy-start | bytes 1540
  23.1 54.5 %copy-start.3 = (bf16[256,512]{1,0:T(8,128)(2,1)S(1)}, bf16[256,512]{1,0:T(8,128)(2,1)}, u32[]{:S(2)}) copy-start(bf16[256,512]{1,0:T(8,128)(2,1)} %constant.18.clone.table_ref) | copy-start | bytes 786436
  23.2 8.0 %collective-permute-start.3 = (bf16[32,2048]{1,0:T(8,128)(2,1)S(1)}, bf16[32,2048]{1,0:T(8,128)(2,1)S(1)}, u32[]{:S(2)}, u32[]{:S(2)}) collective-permute-start(bf16[32,2048]{1,0:T(8,128)(2,1)S(1)} %whiten.1.refs_0_), channel_id=1, source_target_pairs={{4,0},{5,1},{6,2},{7,3},{8,4},{9,5},{10,6},{11,7},{12,8},{13,9},{1... | collective-permute-start | bytes 393224 | tf_op jit(solution)/shard_map/ppermute | solution.py:284
  24.6 8.4 %collective-permute-start.1 = (bf16[32,2048]{1,0:T(8,128)(2,1)S(1)}, bf16[32,2048]{1,0:T(8,128)(2,1)S(1)}, u32[]{:S(2)}, u32[]{:S(2)}) collective-permute-start(bf16[32,2048]{1,0:T(8,128)(2,1)S(1)} %whiten.1.refs_0_), channel_id=1, source_target_pairs={{2,0},{3,1},{4,2},{5,3},{6,4},{7,5},{8,6},{9,7},{10,8},{11,9},{12,... | collective-permute-start | bytes 393224 | tf_op jit(solution)/shard_map/ppermute | solution.py:284
  25.9 7.2 %collective-permute-start = (bf16[32,2048]{1,0:T(8,128)(2,1)S(1)}, bf16[32,2048]{1,0:T(8,128)(2,1)S(1)}, u32[]{:S(2)}, u32[]{:S(2)}) collective-permute-start(bf16[32,2048]{1,0:T(8,128)(2,1)S(1)} %whiten.1.refs_0_), channel_id=1, source_target_pairs={{1,0},{0,1},{3,2},{2,3},{5,4},{4,5},{7,6},{6,7},{9,8},{8,9},{11,10... | collective-permute-start | bytes 393224 | tf_op jit(solution)/shard_map/ppermute | solution.py:285
  31.2 1.9 %collective-permute-start.4 = (bf16[32,2048]{1,0:T(8,128)(2,1)S(1)}, bf16[32,2048]{1,0:T(8,128)(2,1)S(1)}, u32[]{:S(2)}, u32[]{:S(2)}) collective-permute-start(bf16[32,2048]{1,0:T(8,128)(2,1)S(1)} %collective-permute-done.3.refs_4_), channel_id=1, source_target_pairs={{1,0},{0,1},{3,2},{2,3},{5,4},{4,5},{7,6},{6,7},{9,8},{8,9},{11,10... | collective-permute-start | bytes 393224 | tf_op jit(solution)/shard_map/ppermute | solution.py:285
  33.0 1.3 %collective-permute-start.2 = (bf16[32,2048]{1,0:T(8,128)(2,1)S(1)}, bf16[32,2048]{1,0:T(8,128)(2,1)S(1)}, u32[]{:S(2)}, u32[]{:S(2)}) collective-permute-start(bf16[32,2048]{1,0:T(8,128)(2,1)S(1)} %collective-permute-done.1.refs_2_), channel_id=1, source_target_pairs={{1,0},{0,1},{3,2},{2,3},{5,4},{4,5},{7,6},{6,7},{9,8},{8,9},{11,10... | collective-permute-start | bytes 393224 | tf_op jit(solution)/shard_map/ppermute | solution.py:285
